TPU v7x, 32 devices: a whole 2x2x4 slice. The times are simulated.
32 devices in a mesh: zrow: 4 (over z), zcol: 8 (over y, x, core).
Axes of the slice: x: 2, y: 2, z: 4, core: 2. Of those that a mesh axis runs over, the one named last changes fastest.
Arguments:
- state: float32 [64, 8, 32768], P(None, None, ('zrow', 'zcol')), may hold values from -6 to 6
- kernel: float32 [32768], P(('zrow', 'zcol')), may hold values from 0.5 to 5
- blocks: int32 [2048, 4], replicated, may hold values from 0 to 255
- foot_weight: float32 [2048, 4], replicated, may hold values from 0.2 to 1
- bin_response: float32 [2048, 8], replicated, may hold values from 0.1 to 1
- observed: float32 [2048, 64], replicated, may hold values from -6 to 6
- obs_var: float32 [2048], replicated, may hold values from 0.1 to 1
- batch_order: int32 [2048], replicated, may hold values from 0 to 2047, each once
Outputs:
- analysis: float32 [64, 8, 32768], P(None, None, ('zrow', 'zcol'))
- obs_analysis: float32 [2, 64, 1024], P(None, None, ('zrow', 'zcol'))
All inputs are finite; a program needn't handle non-finite values.
Results may differ from a plain program's by a relative error of at most 0.0003.
Values sent between devices are 32-bit elements; how exact they have to be, the bound alone decides.
No kernel may reach another device: no remote copies, remote signals or barrier semaphores. Data moves between devices by JAX's collectives and lax.ppermute only.
A program may use at most 128 MiB of HBM per device.

v0:
```python
import jax
import jax.numpy as jnp
from jax import lax
from jax.sharding import PartitionSpec as P

BLK = 128
P_SIZE = 1024
BATCHES = 2


def shards(state, kernel, blocks, foot_weight, bin_response, observed, obs_var, batch_order):
    members = state.shape[0]
    nbins = state.shape[1]
    cells = state.shape[2]
    nblocks = cells // BLK
    devices = lax.axis_size(("zrow", "zcol"))
    myself = lax.axis_index(("zrow", "zcol"))
    share = P_SIZE // devices
    high = lax.Precision.HIGHEST
    center = jnp.eye(members, dtype=jnp.float32) - 1.0 / members
    ident = jnp.eye(members, dtype=jnp.float32)

    def batch_ids(batch):
        return batch_order[batch * P_SIZE : (batch + 1) * P_SIZE]

    def observe(means, batch):
        chosen = batch_ids(batch)
        local_blocks = blocks[chosen] - myself * nblocks
        onehot = (
            local_blocks[:, :, None] == jnp.arange(nblocks, dtype=jnp.int32)[None, None, :]
        ).astype(jnp.float32)
        spread = jnp.sum(onehot * foot_weight[chosen][:, :, None], axis=1)
        weights = (bin_response[chosen][:, :, None] * spread[:, None, :]).reshape(
            P_SIZE, nbins * nblocks
        )
        return lax.dot_general(
            means.reshape(members, nbins * nblocks),
            weights,
            (((1,), (1,)), ((), ())),
            precision=high,
        )

    block_weighted = state.reshape(members, nbins, nblocks, BLK) * kernel.reshape(nblocks, BLK)
    means = jnp.sum(block_weighted, axis=3) / BLK
    priors = lax.psum_scatter(
        jnp.stack([observe(means, batch) for batch in range(BATCHES)]),
        ("zrow", "zcol"),
        scatter_dimension=2,
        tiled=True,
    )
    total = ident
    self_sums = []
    obs_sums = []
    for batch in range(BATCHES):
        mine = lax.dynamic_slice_in_dim(batch_ids(batch), myself * share, share, 0)
        weighted = priors[batch] / obs_var[mine][None, :]
        self_sums.append(jnp.dot(weighted, priors[batch].T, precision=high))
        obs_sums.append(jnp.dot(weighted, observed[mine], precision=high))
    self_all, obs_all = lax.psum((jnp.stack(self_sums), jnp.stack(obs_sums)), ("zrow", "zcol"))
    for batch in range(BATCHES):
        left = jnp.dot(center, total, precision=high)
        inner = jnp.dot(jnp.dot(left, self_all[batch], precision=high), left.T, precision=high)
        residue = obs_all[batch] - jnp.dot(self_all[batch], total.T, precision=high)
        cross = jnp.dot(left, residue, precision=high)
        factor = jnp.linalg.cholesky((members - 1) * ident + inner)
        gain = jax.scipy.linalg.cho_solve((factor, True), cross)
        total = jnp.dot(ident + jnp.dot(gain.T, center, precision=high), total, precision=high)
    field = jnp.dot(total, state.reshape(members, -1), precision=high).reshape(
        members, nbins, cells
    )
    finals = jnp.einsum("ij,tjp->tip", total, priors, precision=high)
    return (field, finals)


def solution(mesh):
    return jax.shard_map(
        shards,
        mesh=mesh,
        in_specs=(
            P(None, None, ("zrow", "zcol")),
            P(("zrow", "zcol")),
            P(),
            P(),
            P(),
            P(),
            P(),
            P(),
        ),
        out_specs=(P(None, None, ("zrow", "zcol")), P(None, None, ("zrow", "zcol"))),
        check_vma=False,
    )
```

profile of v0, /device:TPU:0, one launch (start us, length us, event | category | flops | bytes accessed | tf_op | source)
XLA Modules:
  0.0 347.9 jit_solution(2390267959956065888)
XLA Ops:
  7.2 0.7 fusion.50
  7.9 1.1 copy.94
  9.1 4.0 %gather_fusion.4 = s32[1024,4]{1,0:T(8,128)} fusion(s32[2048,4]{1,0:T(8,128)S(1)} %copy.94, s32[1024]{0:T(1024)S(1)} %get-tuple-element.24), kind=kCustom, calls=%fused_computation.4 | custom fusion | bytes 36864 | tf_op jit(solution)/shard_map/gather | solution.py:28
  13.1 4.0 %gather_fusion.1 = s32[1024,4]{1,0:T(8,128)} fusion(s32[2048,4]{1,0:T(8,128)S(1)} %copy.94, s32[1024]{0:T(1024)S(1)} %get-tuple-element.23), kind=kCustom, calls=%fused_computation.1 | custom fusion | bytes 36864 | tf_op jit(solution)/shard_map/gather | solution.py:28
  17.1 0.4 copy.96
  17.4 4.0 %gather_fusion.5 = f32[1024,4]{1,0:T(8,128)} fusion(f32[2048,4]{1,0:T(8,128)S(1)} %copy.96, s32[1024]{0:T(1024)S(1)} %get-tuple-element.24), kind=kCustom, calls=%fused_computation.5 | custom fusion | bytes 36864 | tf_op jit(solution)/shard_map/gather | solution.py:32
  21.5 4.0 %gather_fusion.2 = f32[1024,4]{1,0:T(8,128)} fusion(f32[2048,4]{1,0:T(8,128)S(1)} %copy.96, s32[1024]{0:T(1024)S(1)} %get-tuple-element.23), kind=kCustom, calls=%fused_computation.2 | custom fusion | bytes 36864 | tf_op jit(solution)/shard_map/gather | solution.py:32
  25.4 0.3 copy.92
  25.8 4.0 %gather_fusion.3 = f32[1024,8]{1,0:T(8,128)} fusion(f32[2048,8]{1,0:T(8,128)S(1)} %copy.92, s32[1024]{0:T(1024)S(1)} %get-tuple-element.24), kind=kCustom, calls=%fused_computation.3 | custom fusion | bytes 69632 | tf_op jit(solution)/shard_map/gather | solution.py:33
  29.8 4.0 %gather_fusion = f32[1024,8]{1,0:T(8,128)} fusion(f32[2048,8]{1,0:T(8,128)S(1)} %copy.92, s32[1024]{0:T(1024)S(1)} %get-tuple-element.23), kind=kCustom, calls=%fused_computation | custom fusion | bytes 69632 | tf_op jit(solution)/shard_map/gather | solution.py:33
  33.8 0.6 fusion.3
  34.5 1.2 copy.95
  35.8 0.2 copy.101
  36.0 1.2 copy.97
  37.2 0.2 copy.103
  37.4 1.2 copy.93
  38.6 1.2 copy.99
  39.9 0.4 convolution_bitcast_fusion
  40.4 0.4 convolution_bitcast_fusion.1
  40.8 1.3 copy.104
  42.1 0.2 all-reduce.7.cloned.1.call-start
  42.5 0.7 gather_fusion.7
  43.2 0.7 gather_fusion.6
  43.9 1.4 copy.107
  45.2 0.6 gather_fusion.9
  45.8 0.6 gather_fusion.8
  46.4 0.2 fusion.11
  46.6 128.3 %all-reduce.5.cloned.1.call-done = f32[2,64,1024]{1,0,2:T(2,128)} async-done(((f32[2,64,1024]{1,0,2:T(2,128)}), f32[2,64,1024]{1,0,2:T(2,128)}) %all-reduce.5.cloned.1.call-update) | async-done | bytes 524304
  174.9 1.0 broadcast_divide_fusion.1
  175.9 0.2 convolution_bitcast_fusion.7
  176.1 0.3 convolution_bitcast_fusion.5
  176.4 0.2 convolution_bitcast_fusion.6
  176.7 0.3 convolution_bitcast_fusion.4
  177.0 0.6 pad_maximum_fusion.1
  177.6 0.6 pad_maximum_fusion.2
  178.3 0.8 constant_dynamic-slice_fusion.2
  179.0 124.9 %all-reduce.7.cloned.1.call-done = (f32[2,64,64]{2,1,0:T(8,128)}, f32[2,64,64]{2,1,0:T(8,128)}) async-done(((f32[2,64,64]{2,1,0:T(8,128)}, f32[2,64,64]{2,1,0:T(8,128)}), (f32[2,64,64]{2,1,0:T(8,128)}, f32[2,64,64]{2,1,0:T(8,128)})) %all-reduce.7.cloned.1.call-update) | async-done | bytes 65552 | tf_op jit(solution)/shard_map/psum | solution.py:59
  303.9 0.9 convolution_subtract_fusion.1
  304.9 0.9 fusion.28
  305.8 0.2 fusion.51
  306.0 0.2 convolution_add_fusion.3
  306.2 5.8 %cholesky.44 = f32[64,64]{1,0:T(8,128)S(1)} custom-call(f32[64,64]{1,0:T(8,128)S(1)} %fusion.23), custom_call_target="Cholesky" | custom-call | tf_op jit(solution)/shard_map/jit(cholesky)/cholesky | solution.py:65
  312.1 0.6 compare_reduce_fusion.1
  312.8 0.7 fusion.12
  313.4 4.9 %custom-call.8 = f32[1,64,64]{1,2,0:T(8,128)S(1)} custom-call(f32[1,64,64]{2,1,0:T(8,128)S(1)} %fusion.12), custom_call_target="InvertDiagBlocksLowerTriangular" | custom-call | tf_op jit(solution)/shard_map/jit(_cho_solve)/triangular_solve | solution.py:66
  318.3 0.3 fusion.21
  318.8 0.2 convolution_add_fusion.2
  318.9 0.2 fusion.27
  319.1 1.0 convolution_subtract_fusion
  320.1 0.2 fusion.10
  320.4 0.9 fusion.29
  321.3 0.2 convolution_add_fusion.1
  321.5 0.2 fusion.52
  321.7 5.8 %cholesky.55 = f32[64,64]{1,0:T(8,128)S(1)} custom-call(f32[64,64]{1,0:T(8,128)S(1)} %fusion.18), custom_call_target="Cholesky" | custom-call | tf_op jit(solution)/shard_map/jit(cholesky)/cholesky | solution.py:65
  327.6 0.6 compare_reduce_fusion
  328.3 0.7 fusion.13
  328.9 4.9 %custom-call.9 = f32[1,64,64]{1,2,0:T(8,128)S(1)} custom-call(f32[1,64,64]{2,1,0:T(8,128)S(1)} %fusion.13), custom_call_target="InvertDiagBlocksLowerTriangular" | custom-call | tf_op jit(solution)/shard_map/jit(_cho_solve)/triangular_solve | solution.py:66
  333.8 0.3 fusion.16
  334.1 0.2 fusion.14
  334.3 0.2 convolution_add_fusion
  334.4 0.2 convolution_bitcast_fusion.3
  334.7 0.8 convolution_bitcast_fusion.2
  335.5 3.0 fusion
  338.5 2.5 copy.115
  (32 shorter events, 0.8 us)
Async XLA Ops:
  7.2 35.3 %copy-start = (f32[2048]{0:T(1024)S(1)}, f32[2048]{0:T(1024)}, u32[]{:S(2)}) copy-start(f32[2048]{0:T(1024)} %param.17) | copy-start | bytes 24580
  7.2 167.7 %all-reduce.5.cloned.1.call-start = ((), (), s32[]{:S(2)}) async-start(), calls=%async_computation | async-start | bytes 2097152
  13.1 4.0 %copy-start.5 = (f32[2048,4]{0,1:T(4,128)S(1)}, f32[2048,4]{0,1:T(4,128)}, u32[]{:S(2)}) copy-start(f32[2048,4]{0,1:T(4,128)} %param.14) | copy-start | bytes 98308
  21.5 4.0 %copy-start.4 = (f32[2048,8]{0,1:T(8,128)S(1)}, f32[2048,8]{0,1:T(8,128)}, u32[]{:S(2)}) copy-start(f32[2048,8]{0,1:T(8,128)} %param.15) | copy-start | bytes 196612
  29.8 4.0 %copy-start.1 = (f32[64,8,1024]{2,1,0:T(8,128)S(1)}, f32[64,8,1024]{2,1,0:T(8,128)}, u32[]{:S(2)}) copy-start(f32[64,8,1024]{2,1,0:T(8,128)} %param.11) | copy-start | bytes 6291460
  29.8 4.0 %copy-start.6 = (f32[1024]{0:T(1024)S(1)}, f32[1024]{0:T(1024)}, u32[]{:S(2)}) copy-start(f32[1024]{0:T(1024)} %param.12) | copy-start | bytes 12292
  33.8 2.0 copy-start.2
  33.8 3.4 copy-start.3
  42.1 261.8 %all-reduce.7.cloned.1.call-start = ((), (), s32[]{:S(2)}) async-start(), calls=%async_computation.1 | async-start | bytes 262144 | tf_op jit(solution)/shard_map/psum | solution.py:59
Sparse Core Ops, SparseCore 0:
  42.2 132.5 all-reduce.4
  182.1 121.7 all-reduce.6
where the time goes:
time: 349 us; the launch traced here: 348 us
  waiting for transfers between devices  253 us (72%)
  local copies, waits for them, and re-layouts  39.9 us (11%)
  other arithmetic  27.9 us (8%)
  between operations  14.4 us (4%)
  matrix products  12.2 us (3%)
    unnamed x3, waiting for transfers between devices  128 us
    psum x1, waiting for transfers between devices, shards(): lax.psum((jnp.stack(self_sums), jnp.stack(obs_sums)), ('zrow', 'zcol'))  125 us
    another operation x6, other arithmetic, shards(): factor = jnp.linalg.cholesky((members - 1) * ident + inner)  13 us
    another operation x4, other arithmetic, shards(): gain = jax.scipy.linalg.cho_solve((factor, True), cross)  11.1 us
    gather x4, local copies, waits for them, and re-layouts, observe(): bin_response[chosen][:, :, None] * spread[:, None, :]  10.4 us
    gather x4, local copies, waits for them, and re-layouts, observe(): spread = jnp.sum(onehot * foot_weight[chosen][:, :, None], axis=1)  9.45 us
    gather x4, local copies, waits for them, and re-layouts, observe(): local_blocks = blocks[chosen] - myself * nblocks  9.42 us
  transfers between devices with their start and end apart: 2, of which 2 were waited for; matrix products, arithmetic and copies ran while one was open for 1% of the time, Pallas kernels for 0%

commit v1 on v0

--- a/solution.py
+++ b/solution.py
@@ -1,3 +1,4 @@
+import functools
 import jax
 import jax.numpy as jnp
 from jax import lax
@@ -6,6 +7,15 @@
 BLK = 128
 P_SIZE = 1024
 BATCHES = 2
+
+
+def views_open(work_x, device_axis, bus_axis):
+    for w in (device_axis, bus_axis):
+        work_x = lax.psum(work_x, axis_name=w)
+    return work_x
+
+
+serve_target = functools.partial(views_open, device_axis="zcol", bus_axis="zrow")
 
 
 def shards(state, kernel, blocks, foot_weight, bin_response, observed, obs_var, batch_order):
@@ -56,7 +66,7 @@
         weighted = priors[batch] / obs_var[mine][None, :]
         self_sums.append(jnp.dot(weighted, priors[batch].T, precision=high))
         obs_sums.append(jnp.dot(weighted, observed[mine], precision=high))
-    self_all, obs_all = lax.psum((jnp.stack(self_sums), jnp.stack(obs_sums)), ("zrow", "zcol"))
+    self_all, obs_all = serve_target((jnp.stack(self_sums), jnp.stack(obs_sums)))
     for batch in range(BATCHES):
         left = jnp.dot(center, total, precision=high)
         inner = jnp.dot(jnp.dot(left, self_all[batch], precision=high), left.T, precision=high)

time: 349 us -> 312 us (0.89)
  waiting for transfers between devices: 253 us -> 216 us
    psum x1 -> x2, waiting for transfers between devices: 125 us -> 87.6 us  [views_open(): work_x = lax.psum(work_x, axis_name=w)]
    unnamed x3 -> x4, waiting for transfers between devices: 128 us -> 129 us
  transfers between devices with their start and end apart: 2 -> 3, of which waited for: 2 -> 3; matrix products, arithmetic and copies ran while one was open for 1% -> 2% of each run, Pallas kernels for 0% -> 0%
where the time goes in v1:
time: 312 us; the launch traced here: 311 us
  waiting for transfers between devices  216 us (69%)
  local copies, waits for them, and re-layouts  39.9 us (13%)
  other arithmetic  27.9 us (9%)
  between operations  14.1 us (5%)
  matrix products  12.2 us (4%)
    unnamed x4, waiting for transfers between devices  129 us
    psum x2, waiting for transfers between devices, views_open(): work_x = lax.psum(work_x, axis_name=w)  87.6 us
    another operation x6, other arithmetic, shards(): factor = jnp.linalg.cholesky((members - 1) * ident + inner)  13 us
    another operation x4, other arithmetic, shards(): gain = jax.scipy.linalg.cho_solve((factor, True), cross)  11.1 us
    gather x4, local copies, waits for them, and re-layouts, observe(): bin_response[chosen][:, :, None] * spread[:, None, :]  10.4 us
    gather x4, local copies, waits for them, and re-layouts, observe(): spread = jnp.sum(onehot * foot_weight[chosen][:, :, None], axis=1)  9.45 us
    gather x4, local copies, waits for them, and re-layouts, observe(): local_blocks = blocks[chosen] - myself * nblocks  9.42 us
    unnamed x20, local copies, waits for them, and re-layouts  6.51 us
  transfers between devices with their start and end apart: 3, of which 3 were waited for; matrix products, arithmetic and copies ran while one was open for 2% of the time, Pallas kernels for 0%

profile of v1, /device:TPU:0, one launch (start us, length us, event | category | flops | bytes accessed | tf_op | source)
XLA Modules:
  0.0 310.8 jit_solution(9592850189965675017)
XLA Ops:
  7.2 0.7 fusion.50
  7.9 1.1 copy.94
  9.1 4.0 %gather_fusion.4 = s32[1024,4]{1,0:T(8,128)} fusion(s32[2048,4]{1,0:T(8,128)S(1)} %copy.94, s32[1024]{0:T(1024)S(1)} %get-tuple-element.26), kind=kCustom, calls=%fused_computation.4 | custom fusion | bytes 36864 | tf_op jit(solution)/shard_map/gather | solution.py:38
  13.1 4.0 %gather_fusion.1 = s32[1024,4]{1,0:T(8,128)} fusion(s32[2048,4]{1,0:T(8,128)S(1)} %copy.94, s32[1024]{0:T(1024)S(1)} %get-tuple-element.25), kind=kCustom, calls=%fused_computation.1 | custom fusion | bytes 36864 | tf_op jit(solution)/shard_map/gather | solution.py:38
  17.1 0.4 copy.96
  17.4 4.0 %gather_fusion.5 = f32[1024,4]{1,0:T(8,128)} fusion(f32[2048,4]{1,0:T(8,128)S(1)} %copy.96, s32[1024]{0:T(1024)S(1)} %get-tuple-element.26), kind=kCustom, calls=%fused_computation.5 | custom fusion | bytes 36864 | tf_op jit(solution)/shard_map/gather | solution.py:42
  21.5 4.0 %gather_fusion.2 = f32[1024,4]{1,0:T(8,128)} fusion(f32[2048,4]{1,0:T(8,128)S(1)} %copy.96, s32[1024]{0:T(1024)S(1)} %get-tuple-element.25), kind=kCustom, calls=%fused_computation.2 | custom fusion | bytes 36864 | tf_op jit(solution)/shard_map/gather | solution.py:42
  25.4 0.3 copy.92
  25.8 4.0 %gather_fusion.3 = f32[1024,8]{1,0:T(8,128)} fusion(f32[2048,8]{1,0:T(8,128)S(1)} %copy.92, s32[1024]{0:T(1024)S(1)} %get-tuple-element.26), kind=kCustom, calls=%fused_computation.3 | custom fusion | bytes 69632 | tf_op jit(solution)/shard_map/gather | solution.py:43
  29.8 4.0 %gather_fusion = f32[1024,8]{1,0:T(8,128)} fusion(f32[2048,8]{1,0:T(8,128)S(1)} %copy.92, s32[1024]{0:T(1024)S(1)} %get-tuple-element.25), kind=kCustom, calls=%fused_computation | custom fusion | bytes 69632 | tf_op jit(solution)/shard_map/gather | solution.py:43
  33.8 0.6 fusion.3
  34.5 1.2 copy.95
  35.8 0.2 copy.101
  36.0 1.2 copy.97
  37.2 0.2 copy.103
  37.4 1.2 copy.93
  38.6 1.2 copy.99
  39.9 0.4 convolution_bitcast_fusion
  40.4 0.4 convolution_bitcast_fusion.1
  40.8 1.3 copy.104
  42.3 0.7 gather_fusion.7
  43.0 0.7 gather_fusion.6
  43.7 1.4 copy.107
  45.1 0.6 gather_fusion.9
  45.6 0.6 gather_fusion.8
  46.2 128.7 %all-reduce.7.cloned.1.call-done = f32[2,64,1024]{1,0,2:T(2,128)} async-done(((f32[2,64,1024]{1,0,2:T(2,128)}), f32[2,64,1024]{1,0,2:T(2,128)}) %all-reduce.7.cloned.1.call-update) | async-done | bytes 524304
  174.9 1.0 broadcast_divide_fusion.1
  175.9 0.2 convolution_bitcast_fusion.7
  176.1 0.3 convolution_bitcast_fusion.5
  176.4 0.2 convolution_bitcast_fusion.6
  176.7 0.3 convolution_bitcast_fusion.4
  177.0 0.6 pad_maximum_fusion.1
  177.6 0.6 pad_maximum_fusion.2
  178.3 0.2 all-reduce.11.cloned.1.call-start
  178.5 0.2 fusion.11
  178.7 52.2 %all-reduce.9.cloned.1.call-done = (f32[2,64,64]{2,1,0:T(8,128)}, f32[2,64,64]{2,1,0:T(8,128)}) async-done(((f32[2,64,64]{2,1,0:T(8,128)}, f32[2,64,64]{2,1,0:T(8,128)}), (f32[2,64,64]{2,1,0:T(8,128)}, f32[2,64,64]{2,1,0:T(8,128)})) %all-reduce.9.cloned.1.call-update) | async-done | bytes 65552 | tf_op jit(solution)/shard_map/psum | solution.py:14
  230.9 0.8 constant_dynamic-slice_fusion.2
  231.7 35.5 %all-reduce.11.cloned.1.call-done = (f32[2,64,64]{2,1,0:T(8,128)}, f32[2,64,64]{2,1,0:T(8,128)}) async-done(((f32[2,64,64]{2,1,0:T(8,128)}, f32[2,64,64]{2,1,0:T(8,128)}), (f32[2,64,64]{2,1,0:T(8,128)}, f32[2,64,64]{2,1,0:T(8,128)})) %all-reduce.11.cloned.1.call-update) | async-done | bytes 65552 | tf_op jit(solution)/shard_map/psum | solution.py:14
  267.1 0.9 convolution_subtract_fusion.1
  268.1 0.9 fusion.28
  269.2 0.2 convolution_add_fusion.3
  269.5 5.8 %cholesky.44 = f32[64,64]{1,0:T(8,128)S(1)} custom-call(f32[64,64]{1,0:T(8,128)S(1)} %fusion.23), custom_call_target="Cholesky" | custom-call | tf_op jit(solution)/shard_map/jit(cholesky)/cholesky | solution.py:75
  275.3 0.6 compare_reduce_fusion.1
  276.0 0.7 fusion.12
  276.6 4.9 %custom-call.8 = f32[1,64,64]{1,2,0:T(8,128)S(1)} custom-call(f32[1,64,64]{2,1,0:T(8,128)S(1)} %fusion.12), custom_call_target="InvertDiagBlocksLowerTriangular" | custom-call | tf_op jit(solution)/shard_map/jit(_cho_solve)/triangular_solve | solution.py:76
  281.5 0.3 fusion.21
  281.8 0.2 fusion.19
  282.0 0.2 convolution_add_fusion.2
  282.1 0.2 fusion.27
  282.4 1.0 convolution_subtract_fusion
  283.3 0.2 fusion.10
  283.6 0.9 fusion.29
  284.5 0.2 convolution_add_fusion.1
  284.7 0.2 fusion.52
  285.0 5.8 %cholesky.55 = f32[64,64]{1,0:T(8,128)S(1)} custom-call(f32[64,64]{1,0:T(8,128)S(1)} %fusion.18), custom_call_target="Cholesky" | custom-call | tf_op jit(solution)/shard_map/jit(cholesky)/cholesky | solution.py:75
  290.8 0.6 compare_reduce_fusion
  291.5 0.7 fusion.13
  292.1 4.9 %custom-call.9 = f32[1,64,64]{1,2,0:T(8,128)S(1)} custom-call(f32[1,64,64]{2,1,0:T(8,128)S(1)} %fusion.13), custom_call_target="InvertDiagBlocksLowerTriangular" | custom-call | tf_op jit(solution)/shard_map/jit(_cho_solve)/triangular_solve | solution.py:76
  297.0 0.3 fusion.16
  297.5 0.2 convolution_add_fusion
  297.6 0.2 convolution_bitcast_fusion.3
  297.9 0.8 convolution_bitcast_fusion.2
  298.7 3.0 fusion
  301.7 2.5 copy.115
  (35 shorter events, 1.0 us)
Async XLA Ops:
  7.2 35.1 %copy-start = (f32[2048]{0:T(1024)S(1)}, f32[2048]{0:T(1024)}, u32[]{:S(2)}) copy-start(f32[2048]{0:T(1024)} %param.17) | copy-start | bytes 24580
  7.2 167.7 %all-reduce.7.cloned.1.call-start = ((), (), s32[]{:S(2)}) async-start(), calls=%async_computation | async-start | bytes 2097152
  13.1 4.0 %copy-start.5 = (f32[2048,4]{0,1:T(4,128)S(1)}, f32[2048,4]{0,1:T(4,128)}, u32[]{:S(2)}) copy-start(f32[2048,4]{0,1:T(4,128)} %param.14) | copy-start | bytes 98308
  21.5 4.0 %copy-start.4 = (f32[2048,8]{0,1:T(8,128)S(1)}, f32[2048,8]{0,1:T(8,128)}, u32[]{:S(2)}) copy-start(f32[2048,8]{0,1:T(8,128)} %param.15) | copy-start | bytes 196612
  29.8 4.0 %copy-start.1 = (f32[64,8,1024]{2,1,0:T(8,128)S(1)}, f32[64,8,1024]{2,1,0:T(8,128)}, u32[]{:S(2)}) copy-start(f32[64,8,1024]{2,1,0:T(8,128)} %param.11) | copy-start | bytes 6291460
  29.8 4.0 %copy-start.6 = (f32[1024]{0:T(1024)S(1)}, f32[1024]{0:T(1024)}, u32[]{:S(2)}) copy-start(f32[1024]{0:T(1024)} %param.12) | copy-start | bytes 12292
  33.8 2.0 copy-start.2
  33.8 3.4 %copy-start.3 = (f32[1024,4]{1,0:T(8,128)S(1)}, f32[1024,4]{1,0:T(8,128)}, u32[]{:S(2)}) copy-start(f32[1024,4]{1,0:T(8,128)} %gather_fusion.5) | copy-start | bytes 49156
  42.1 188.7 %all-reduce.9.cloned.1.call-start = ((), (), s32[]{:S(2)}) async-start(), calls=%async_computation.1 | async-start | bytes 262144 | tf_op jit(solution)/shard_map/psum | solution.py:14
  178.3 88.9 %all-reduce.11.cloned.1.call-start = ((), (), s32[]{:S(2)}) async-start(), calls=%async_computation.2 | async-start | bytes 262144 | tf_op jit(solution)/shard_map/psum | solution.py:14
Sparse Core Ops, SparseCore 0:
  42.2 132.5 all-reduce.6
  178.8 51.9 all-reduce.8
  233.2 33.8 all-reduce.10
